TPU v7x, 32 devices: a whole 2x2x4 slice. The times are simulated.
32 devices in a mesh: dp: 4 (over z), blk: 4 (over x, core), seq: 2 (over y).
Axes of the slice: x: 2, y: 2, z: 4, core: 2. Of those that a mesh axis runs over, the one named last changes fastest.
Arguments:
- inputs: bfloat16 [4096, 2304], P(('dp', 'blk', 'seq')), may hold values from -6 to 6
- teacher: bfloat16 [4096, 2304], P(('dp', 'blk', 'seq')), may hold values from -6 to 6
- valid_mask: int32 [4096], replicated, may hold values 0 or 1
- doc_lengths: int32 [4, 8], replicated, may hold values from 1 to 512, 1024 in all within a row
- gain_pre_attention: bfloat16 [2304], P(('dp', 'blk', 'seq')), may hold values from 0.099609375 to 1.8984375
- query_weight: bfloat16 [2304, 2048], P(('dp', 'blk'), 'seq'), may hold values from -0.125 to 0.125
- key_weight: bfloat16 [2304, 1024], P(('dp', 'blk', 'seq')), may hold values from -0.125 to 0.125
- value_weight: bfloat16 [2304, 1024], P(('dp', 'blk', 'seq')), may hold values from -0.125 to 0.125
- output_weight: bfloat16 [2048, 2304], P('seq', ('dp', 'blk')), may hold values from -0.125 to 0.125
- gain_post_attention: bfloat16 [2304], P(('dp', 'blk', 'seq')), may hold values from 0.099609375 to 1.8984375
- gain_pre_feed: bfloat16 [2304], P(('dp', 'blk', 'seq')), may hold values from 0.099609375 to 1.8984375
- gate_weight: bfloat16 [2304, 9216], P(('dp', 'blk'), 'seq'), may hold values from -0.125 to 0.125
- up_weight: bfloat16 [2304, 9216], P(('dp', 'blk'), 'seq'), may hold values from -0.125 to 0.125
- down_weight: bfloat16 [9216, 2304], P('seq', ('dp', 'blk')), may hold values from -0.0625 to 0.0625
- gain_post_feed: bfloat16 [2304], P(('dp', 'blk', 'seq')), may hold values from 0.099609375 to 1.8984375
Outputs:
- layer_output: bfloat16 [4096, 2304], P(('dp', 'blk', 'seq'))
- teacher_loss: float32 [], replicated
- inputs_gradient: float32 [4096, 2304], P(('dp', 'blk', 'seq'))
- gain_pre_attention_gradient: float32 [2304], P(('dp', 'blk', 'seq'))
- query_weight_gradient: float32 [2304, 2048], P(('dp', 'blk'), 'seq')
- key_weight_gradient: float32 [2304, 1024], P(('dp', 'blk', 'seq'))
- value_weight_gradient: float32 [2304, 1024], P(('dp', 'blk', 'seq'))
- output_weight_gradient: float32 [2048, 2304], P('seq', ('dp', 'blk'))
- gain_post_attention_gradient: float32 [2304], P(('dp', 'blk', 'seq'))
- gain_pre_feed_gradient: float32 [2304], P(('dp', 'blk', 'seq'))
- gate_weight_gradient: float32 [2304, 9216], P(('dp', 'blk'), 'seq')
- up_weight_gradient: float32 [2304, 9216], P(('dp', 'blk'), 'seq')
- down_weight_gradient: float32 [9216, 2304], P('seq', ('dp', 'blk'))
- gain_post_feed_gradient: float32 [2304], P(('dp', 'blk', 'seq'))
Inputs may be any that keep to these rules, and one draw needn't show every extreme that they name: `doc_lengths`: each row fills one sequence of 1024 tokens; its last span is padding; the largest entry of each row is exactly 512.
All inputs are finite; a program needn't handle non-finite values.
Results may differ from a plain program's by a relative error of at most 0.02.
Values may be sent and summed in bfloat16 or wider, within the bound.
A program may use at most 320 MiB of HBM per device.

v0:
```python
import jax
import jax.numpy as jnp
from jax import lax
from jax.sharding import PartitionSpec as P

HQ = 8
KVH = 4
HD = 256


EPS = 1e-06
CAP = 50.0
SCALE = 0.0625
NEG = -1e30


def segment_ids(lengths, total_rows):
    ends_at = jnp.cumsum(lengths)
    places = jnp.arange(total_rows, dtype=jnp.int32)
    number = jnp.sum((places[:, None] >= ends_at[None, :]).astype(jnp.int32), axis=1)
    return jnp.where(number == lengths.shape[0] - 1, -1, number)


def scale_rows(source, gain):
    inverse = lax.rsqrt(jnp.mean(source * source, axis=-1, keepdims=True) + EPS)
    return (source * inverse * gain, inverse)


def scale_back(source, inverse, gain, upstream):
    weighted = upstream * gain
    inner_mean = jnp.mean(weighted * source, axis=-1, keepdims=True)
    grad_source = inverse * weighted - source * (inverse * inverse * inverse) * inner_mean
    grad_gain = jnp.sum(upstream * source * inverse, axis=0)
    return (grad_source, grad_gain)


def inner_rows(left_side, right_side):
    return lax.dot_general(
        left_side, right_side, (((0,), (0,)), ((), ())), preferred_element_type=jnp.float32
    )


def against(left_side, right_side):
    return lax.dot_general(
        left_side, right_side, (((1,), (1,)), ((), ())), preferred_element_type=jnp.float32
    )


def geglu(gate_value, up_value):
    return jax.nn.gelu(gate_value, approximate=True) * up_value


def fetch_weights(
    gain_pre_attention,
    key_weight,
    value_weight,
    gain_post_attention,
    gain_pre_feed,
    gain_post_feed,
    gate_weight,
    up_weight,
    down_weight,
    query_weight,
    output_weight,
):
    small_set = (
        lax.all_gather(gain_pre_attention, ("dp", "blk", "seq"), axis=0, tiled=True),
        lax.all_gather(key_weight, ("dp", "blk", "seq"), axis=0, tiled=True),
        lax.all_gather(value_weight, ("dp", "blk", "seq"), axis=0, tiled=True),
        lax.all_gather(gain_post_attention, ("dp", "blk", "seq"), axis=0, tiled=True),
        lax.all_gather(gain_pre_feed, ("dp", "blk", "seq"), axis=0, tiled=True),
        lax.all_gather(gain_post_feed, ("dp", "blk", "seq"), axis=0, tiled=True),
    )
    feed_set = (
        lax.all_gather(gate_weight, ("dp", "blk"), axis=0, tiled=True),
        lax.all_gather(up_weight, ("dp", "blk"), axis=0, tiled=True),
        lax.all_gather(down_weight, ("dp", "blk"), axis=1, tiled=True),
        lax.all_gather(query_weight, ("dp", "blk"), axis=0, tiled=True),
        lax.all_gather(output_weight, ("dp", "blk"), axis=1, tiled=True),
    )
    head_set = (
        lax.all_gather(feed_set[3], "seq", axis=1, tiled=True),
        lax.all_gather(feed_set[4], "seq", axis=0, tiled=True),
    )
    return (small_set, feed_set, head_set)


def block_gather(rows_here):
    return lax.all_gather(rows_here, "seq", axis=0, tiled=True)


def block_sum(term, own_rows):
    return lax.psum_scatter(
        term(jnp.int32(0), own_rows * lax.axis_size("seq")), "seq", scatter_dimension=0, tiled=True
    )


def to_heads(members):
    return (
        lax.all_to_all(members[0], "seq", split_axis=1, concat_axis=0, tiled=True),
        lax.all_to_all(members[1], "seq", split_axis=1, concat_axis=0, tiled=True),
        lax.all_to_all(members[2], "seq", split_axis=1, concat_axis=0, tiled=True),
    )


def to_rows(members):
    return (
        lax.all_to_all(members[0], "seq", split_axis=0, concat_axis=1, tiled=True),
        lax.all_to_all(members[1], "seq", split_axis=0, concat_axis=1, tiled=True),
        lax.all_to_all(members[2], "seq", split_axis=0, concat_axis=1, tiled=True),
    )


def shards(
    inputs,
    teacher,
    valid_mask,
    doc_lengths,
    gain_pre_attention,
    query_weight,
    key_weight,
    value_weight,
    output_weight,
    gain_post_attention,
    gain_pre_feed,
    gate_weight,
    up_weight,
    down_weight,
    gain_post_feed,
):
    seq_size = lax.axis_size("seq")
    cycle_size = lax.axis_size("blk")
    devices_all = lax.axis_size("dp") * cycle_size * seq_size
    own_rows = inputs.shape[0]
    width = inputs.shape[1]
    block_rows = own_rows * seq_size
    seq_length = block_rows * cycle_size
    heads_here = HQ // seq_size
    kv_total = max(KVH, seq_size)
    repeats = kv_total // KVH
    kv_here = kv_total // seq_size
    group_size = heads_here // kv_here
    query_rows = min(512, block_rows)
    query_blocks = block_rows // query_rows
    cycle_index = lax.axis_index("blk")
    seq_index = lax.axis_index("seq")
    data_index = lax.axis_index("dp")
    seg_every = jax.vmap(lambda row_lengths: segment_ids(row_lengths, seq_length))(doc_lengths)
    live_every = ((valid_mask.reshape(seg_every.shape) == 1) & (seg_every >= 0)).reshape(-1)
    count = jnp.maximum(jnp.sum(live_every.astype(jnp.float32)), 1.0)
    token_total = float(seg_every.size)
    seg_all = lax.dynamic_index_in_dim(seg_every, data_index, 0, keepdims=False)
    block_first = cycle_index * block_rows
    own_first = block_first + seq_index * own_rows
    seg_block = lax.dynamic_slice_in_dim(seg_all, block_first, block_rows)
    live_own = lax.dynamic_slice_in_dim(live_every, data_index * seq_length + own_first, own_rows)
    small_set, feed_set, head_set = fetch_weights(
        gain_pre_attention,
        key_weight,
        value_weight,
        gain_post_attention,
        gain_pre_feed,
        gain_post_feed,
        gate_weight,
        up_weight,
        down_weight,
        query_weight,
        output_weight,
    )
    gain_first = small_set[0].astype(jnp.float32)
    gain_second = small_set[3].astype(jnp.float32)
    gain_third = small_set[4].astype(jnp.float32)
    gain_fourth = small_set[5].astype(jnp.float32)
    source = inputs.astype(jnp.float32)
    normed_attention, inverse_one = scale_rows(source, gain_first)
    attention_in = normed_attention.astype(jnp.bfloat16)
    keys_own = (
        jnp.dot(attention_in, small_set[1], preferred_element_type=jnp.float32)
        .astype(jnp.bfloat16)
        .reshape(own_rows, KVH, HD)
    )
    values_own = (
        jnp.dot(attention_in, small_set[2], preferred_element_type=jnp.float32)
        .astype(jnp.bfloat16)
        .reshape(own_rows, KVH, HD)
    )
    if repeats > 1:
        keys_own = jnp.repeat(keys_own, repeats, axis=1)
        values_own = jnp.repeat(values_own, repeats, axis=1)
    queries = (
        jnp.dot(attention_in, head_set[0], preferred_element_type=jnp.float32)
        .astype(jnp.bfloat16)
        .reshape(own_rows, HQ, HD)
    )
    queries_heads, keys_heads, values_heads = to_heads((queries, keys_own, values_own))
    keys_all, values_all = (
        lax.all_gather(keys_heads, "blk", axis=0, tiled=True),
        lax.all_gather(values_heads, "blk", axis=0, tiled=True),
    )
    queries_group = queries_heads.reshape(block_rows, kv_here, group_size, HD)
    positions = block_first + jnp.arange(block_rows, dtype=jnp.int32)
    key_places = jnp.arange(seq_length, dtype=jnp.int32)

    def scores_for(number):
        first_row = number * query_rows
        rows_query = lax.dynamic_slice_in_dim(queries_group, first_row, query_rows)
        rows_place = lax.dynamic_slice_in_dim(positions, first_row, query_rows)
        rows_seg = lax.dynamic_slice_in_dim(seg_block, first_row, query_rows)
        raw_scores = (
            jnp.einsum("qgjd,kgd->qgjk", rows_query, keys_all, preferred_element_type=jnp.float32)
            * SCALE
        )
        capped = CAP * jnp.tanh(raw_scores / CAP)
        allowed = (
            (key_places[None, :] <= rows_place[:, None])
            & (seg_all[None, :] == rows_seg[:, None])
            & ((seg_all[None, :] >= 0) | (key_places[None, :] == rows_place[:, None]))
        )
        return (rows_query, capped, allowed[:, None, None, :])

    def forward_rows(number):
        rows_query, capped, allowed = scores_for(number)
        masked = jnp.where(allowed, capped, NEG)
        highest = jnp.max(masked, axis=-1, keepdims=True)
        weights = jnp.where(allowed, jnp.exp(masked - highest), 0.0)
        totals = jnp.sum(weights, axis=-1, keepdims=True)
        probs = (weights / totals).astype(jnp.bfloat16)
        mixed_rows = jnp.einsum(
            "qgjk,kgd->qgjd", probs, values_all, preferred_element_type=jnp.float32
        )
        return (mixed_rows.astype(jnp.bfloat16), (highest + jnp.log(totals))[..., 0])

    mixed_blocks, log_totals = lax.map(forward_rows, jnp.arange(query_blocks, dtype=jnp.int32))
    mixed_heads = mixed_blocks.reshape(block_rows, heads_here, HD)
    mixed_own = lax.all_to_all(mixed_heads, "seq", split_axis=0, concat_axis=1, tiled=True).reshape(
        own_rows, HQ * HD
    )
    branch_attention = jnp.dot(mixed_own, head_set[1], preferred_element_type=jnp.float32)
    normed_branch, inverse_two = scale_rows(branch_attention, gain_second)
    hidden_state = source + normed_branch
    normed_feed, inverse_three = scale_rows(hidden_state, gain_third)
    feed_in = normed_feed.astype(jnp.bfloat16)
    feed_rows = block_gather(feed_in)
    gate_value = jnp.dot(feed_rows, feed_set[0], preferred_element_type=jnp.float32)
    up_value = jnp.dot(feed_rows, feed_set[1], preferred_element_type=jnp.float32)
    product_rows = geglu(gate_value, up_value).astype(jnp.bfloat16)
    down_forward = feed_set[2]

    def feed_term(first_row, count_rows):
        return jnp.dot(product_rows, down_forward, preferred_element_type=jnp.float32)

    branch_feed = block_sum(feed_term, own_rows)
    normed_out, inverse_four = scale_rows(branch_feed, gain_fourth)
    layer_rows = hidden_state + normed_out
    difference = jnp.where(live_own[:, None], layer_rows - teacher.astype(jnp.float32), 0.0)
    error_own = jnp.sum(difference * difference)
    upstream = difference * (2.0 * token_total / count)
    back_small, back_feed, back_head = fetch_weights(
        gain_pre_attention,
        key_weight,
        value_weight,
        gain_post_attention,
        gain_pre_feed,
        gain_post_feed,
        gate_weight,
        up_weight,
        down_weight,
        query_weight,
        output_weight,
    )
    grad_branch_feed, grad_gain_four = scale_back(branch_feed, inverse_four, gain_fourth, upstream)
    feed_grad_rows = block_gather(grad_branch_feed.astype(jnp.bfloat16))
    grad_product = against(feed_grad_rows, back_feed[2])
    grad_down_local = inner_rows(product_rows, feed_grad_rows)
    geglu_value, geglu_pull = jax.vjp(geglu, gate_value, up_value)
    grad_gate_value, grad_up_value = geglu_pull(grad_product)
    gate_back = grad_gate_value.astype(jnp.bfloat16)
    up_back = grad_up_value.astype(jnp.bfloat16)
    grad_gate_local = inner_rows(feed_rows, gate_back)
    grad_up_local = inner_rows(feed_rows, up_back)
    gate_matrix = back_feed[0]
    up_matrix = back_feed[1]

    def feed_back_term(first_row, count_rows):
        return against(gate_back, gate_matrix) + against(up_back, up_matrix)

    grad_feed_in = block_sum(feed_back_term, own_rows)
    grad_hidden_part, grad_gain_three = scale_back(
        hidden_state, inverse_three, gain_third, grad_feed_in
    )
    grad_hidden = upstream + grad_hidden_part
    grad_branch_attention, grad_gain_two = scale_back(
        branch_attention, inverse_two, gain_second, grad_hidden
    )
    branch_back = grad_branch_attention.astype(jnp.bfloat16)
    grad_output_local = inner_rows(mixed_own, branch_back)
    mixed_back = against(branch_back, back_head[1]).astype(jnp.bfloat16).reshape(own_rows, HQ, HD)
    mixed_back_heads = lax.all_to_all(
        mixed_back, "seq", split_axis=1, concat_axis=0, tiled=True
    ).reshape(block_rows, kv_here, group_size, HD)

    def backward_rows(key_terms, number):
        rows_query, capped, allowed = scores_for(number)
        first_row = number * query_rows
        rows_grad = lax.dynamic_slice_in_dim(mixed_back_heads, first_row, query_rows)
        rows_log = log_totals[number]
        probs = jnp.where(allowed, jnp.exp(capped - rows_log[..., None]), 0.0)
        grad_probs = jnp.einsum(
            "qgjd,kgd->qgjk", rows_grad, values_all, preferred_element_type=jnp.float32
        )
        centre = jnp.sum(probs * grad_probs, axis=-1, keepdims=True)
        score_back = (probs * (grad_probs - centre) * (1.0 - capped / CAP * (capped / CAP))).astype(
            jnp.bfloat16
        )
        grad_rows = (
            jnp.einsum("qgjk,kgd->qgjd", score_back, keys_all, preferred_element_type=jnp.float32)
            * SCALE
        )
        grad_keys = (
            jnp.einsum("qgjk,qgjd->kgd", score_back, rows_query, preferred_element_type=jnp.float32)
            * SCALE
        )
        grad_values = jnp.einsum(
            "qgjk,qgjd->kgd",
            probs.astype(jnp.bfloat16),
            rows_grad,
            preferred_element_type=jnp.float32,
        )
        return (
            key_terms + jnp.concatenate([grad_keys, grad_values], axis=-1),
            grad_rows.astype(jnp.bfloat16),
        )

    key_terms, grad_query_blocks = lax.scan(
        backward_rows,
        jnp.zeros((seq_length, kv_here, 2 * HD), jnp.float32),
        jnp.arange(query_blocks, dtype=jnp.int32),
    )
    key_sums = lax.psum_scatter(
        key_terms.astype(jnp.bfloat16), "blk", scatter_dimension=0, tiled=True
    ).astype(jnp.float32)
    grad_keys_heads = key_sums[..., :HD].astype(jnp.bfloat16)
    grad_values_heads = key_sums[..., HD:].astype(jnp.bfloat16)
    grad_queries_heads = grad_query_blocks.reshape(block_rows, heads_here, HD)
    grad_queries, grad_keys_own, grad_values_own = to_rows(
        (grad_queries_heads, grad_keys_heads, grad_values_heads)
    )
    if repeats > 1:
        grad_keys_own = jnp.sum(
            grad_keys_own.astype(jnp.float32).reshape(own_rows, KVH, repeats, HD), axis=2
        ).astype(jnp.bfloat16)
        grad_values_own = jnp.sum(
            grad_values_own.astype(jnp.float32).reshape(own_rows, KVH, repeats, HD), axis=2
        ).astype(jnp.bfloat16)
    key_back = grad_keys_own.reshape(own_rows, KVH * HD)
    value_back = grad_values_own.reshape(own_rows, KVH * HD)
    kv_back = against(key_back, back_small[1]) + against(value_back, back_small[2])
    query_back = grad_queries.reshape(own_rows, HQ * HD)
    attention_back = against(query_back, back_head[0]) + kv_back
    grad_query_local = inner_rows(attention_in, query_back)
    query_sum, output_sum = (
        lax.psum_scatter(
            grad_query_local.astype(jnp.bfloat16), "seq", scatter_dimension=1, tiled=True
        ).astype(jnp.float32),
        lax.psum_scatter(
            grad_output_local.astype(jnp.bfloat16), "seq", scatter_dimension=0, tiled=True
        ).astype(jnp.float32),
    )
    grad_key_local = inner_rows(attention_in, key_back)
    grad_value_local = inner_rows(attention_in, value_back)
    grad_source, grad_gain_one = scale_back(source, inverse_one, gain_first, attention_back)
    inputs_gradient = grad_hidden + grad_source
    error_slots = jnp.full((devices_all,), error_own, jnp.float32)
    summed = (
        lax.psum_scatter(grad_gain_one, ("dp", "blk", "seq"), scatter_dimension=0, tiled=True),
        lax.psum_scatter(grad_key_local, ("dp", "blk", "seq"), scatter_dimension=0, tiled=True),
        lax.psum_scatter(grad_value_local, ("dp", "blk", "seq"), scatter_dimension=0, tiled=True),
        lax.psum_scatter(grad_gain_two, ("dp", "blk", "seq"), scatter_dimension=0, tiled=True),
        lax.psum_scatter(grad_gain_three, ("dp", "blk", "seq"), scatter_dimension=0, tiled=True),
        lax.psum_scatter(grad_gain_four, ("dp", "blk", "seq"), scatter_dimension=0, tiled=True),
        lax.psum_scatter(error_slots, ("dp", "blk", "seq"), scatter_dimension=0, tiled=True),
    )
    feed_summed = (
        lax.psum_scatter(
            grad_gate_local.astype(jnp.bfloat16), ("dp", "blk"), scatter_dimension=0, tiled=True
        ).astype(jnp.float32),
        lax.psum_scatter(
            grad_up_local.astype(jnp.bfloat16), ("dp", "blk"), scatter_dimension=0, tiled=True
        ).astype(jnp.float32),
        lax.psum_scatter(
            grad_down_local.astype(jnp.bfloat16), ("dp", "blk"), scatter_dimension=1, tiled=True
        ).astype(jnp.float32),
        lax.psum_scatter(
            query_sum.astype(jnp.bfloat16), ("dp", "blk"), scatter_dimension=0, tiled=True
        ).astype(jnp.float32),
        lax.psum_scatter(
            output_sum.astype(jnp.bfloat16), ("dp", "blk"), scatter_dimension=1, tiled=True
        ).astype(jnp.float32),
    )
    loss_value = summed[6][0] / (width * count)
    layer_output = layer_rows.astype(jnp.bfloat16)
    return (
        layer_output,
        loss_value,
        inputs_gradient,
        summed[0],
        feed_summed[3],
        summed[1],
        summed[2],
        feed_summed[4],
        summed[3],
        summed[4],
        feed_summed[0],
        feed_summed[1],
        feed_summed[2],
        summed[5],
    )


def solution(mesh):
    in_specs = (
        P(("dp", "blk", "seq"), None),
        P(("dp", "blk", "seq"), None),
        P(),
        P(),
        P(("dp", "blk", "seq")),
        P(("dp", "blk"), "seq"),
        P(("dp", "blk", "seq"), None),
        P(("dp", "blk", "seq"), None),
        P("seq", ("dp", "blk")),
        P(("dp", "blk", "seq")),
        P(("dp", "blk", "seq")),
        P(("dp", "blk"), "seq"),
        P(("dp", "blk"), "seq"),
        P("seq", ("dp", "blk")),
        P(("dp", "blk", "seq")),
    )
    out_specs = (
        P(("dp", "blk", "seq"), None),
        P(),
        P(("dp", "blk", "seq"), None),
        P(("dp", "blk", "seq")),
        P(("dp", "blk"), "seq"),
        P(("dp", "blk", "seq"), None),
        P(("dp", "blk", "seq"), None),
        P("seq", ("dp", "blk")),
        P(("dp", "blk", "seq")),
        P(("dp", "blk", "seq")),
        P(("dp", "blk"), "seq"),
        P(("dp", "blk"), "seq"),
        P("seq", ("dp", "blk")),
        P(("dp", "blk", "seq")),
    )
    return jax.shard_map(shards, mesh=mesh, in_specs=in_specs, out_specs=out_specs, check_vma=False)
```

profile of v0, /device:TPU:0, one launch (start us, length us, event | category | flops | bytes accessed | tf_op | source)
XLA Modules:
  0.0 2425.1 jit_solution(1335151790093959574)
XLA Ops:
  10.1 56.1 %all-gather.22.cloned.1.call-done = bf16[2304,1024]{1,0:T(8,128)(2,1)} async-done(((bf16[144,1024]{1,0:T(8,128)(2,1)}), bf16[2304,1024]{1,0:T(8,128)(2,1)}) %all-gather.22.cloned.1.call-update) | async-done | bytes 4718608 | tf_op jit(solution)/shard_map/all_gather | solution.py:78
  67.3 39.9 %all-reduce.10 = (bf16[2304]{0:T(1024)(128)(2,1)S(1)}, bf16[2304]{0:T(1024)(128)(2,1)S(1)}, bf16[2304]{0:T(1024)(128)(2,1)S(1)}, bf16[2304]{0:T(1024)(128)(2,1)S(1)}) all-reduce(bf16[2304]{0:T(1024)(128)(2,1)S(1)} %dynamic-update-slice, ...), channel_id=1, replica_groups=mesh['dp'=4,'blk'=4,'seq'=2] {'dp','blk','seq'}, use_global_device_ids=true, to_apply=%add | all-reduce | flops 9216 | bytes 36864
  107.9 23.4 all-gather.18.cloned.1.call-done
  134.5 8.2 all_to_all.126
  143.5 52.6 %all-gather.14.cloned.1.call-done = bf16[2304,1024]{1,0:T(8,128)(2,1)} async-done(((bf16[72,1024]{1,0:T(8,128)(2,1)}), bf16[2304,1024]{1,0:T(8,128)(2,1)}) %all-gather.14.cloned.1.call-update) | async-done | bytes 4718608 | tf_op jit(solution)/shard_map/all_gather | solution.py:69
  199.4 8.2 all_to_all.127
  208.7 41.0 %all-gather.26.cloned.1.call-done = bf16[1024,2304]{0,1:T(8,128)(2,1)} async-done(((bf16[1024,144]{0,1:T(8,128)(2,1)}), bf16[1024,2304]{0,1:T(8,128)(2,1)}) %all-gather.26.cloned.1.call-update) | async-done | bytes 4718608 | tf_op jit(solution)/shard_map/all_gather | solution.py:79
  250.1 117.6 %all-gather.24.cloned.1.call-done = bf16[2304,2048]{1,0:T(8,128)(2,1)} async-done(((bf16[2304,1024]{1,0:T(8,128)(2,1)}), bf16[2304,2048]{1,0:T(8,128)(2,1)}) %all-gather.24.cloned.1.call-update) | async-done | bytes 9437200 | tf_op jit(solution)/shard_map/all_gather | solution.py:82
  378.1 7.2 all-to-all-done.2
  392.2 13.2 all-gather.16.cloned.1.call-done
  414.7 8.4 all-to-all-done.3
  423.4 101.7 %all-gather.28.cloned.1.call-done = bf16[2048,2304]{0,1:T(8,128)(2,1)} async-done(((bf16[1024,2304]{0,1:T(8,128)(2,1)}), bf16[2048,2304]{0,1:T(8,128)(2,1)}) %all-gather.28.cloned.1.call-update) | async-done | bytes 9437200 | tf_op jit(solution)/shard_map/all_gather | solution.py:83
  525.0 7.0 multiply_reduce_fusion.9
  536.9 20.9 all-gather.30.cloned.1.call-done
  557.8 111.5 %all-gather.32.cloned.1.call-done = bf16[2304,4608]{1,0:T(8,128)(2,1)} async-done(((bf16[144,4608]{1,0:T(8,128)(2,1)}), bf16[2304,4608]{1,0:T(8,128)(2,1)}) %all-gather.32.cloned.1.call-update) | async-done | bytes 21233680 | tf_op jit(solution)/shard_map/all_gather | solution.py:75
  669.3 11.7 fusion.106
  681.0 99.9 %all-gather.34.cloned.1.call-done = bf16[2304,4608]{1,0:T(8,128)(2,1)} async-done(((bf16[144,4608]{1,0:T(8,128)(2,1)}), bf16[2304,4608]{1,0:T(8,128)(2,1)}) %all-gather.34.cloned.1.call-update) | async-done | bytes 21233680 | tf_op jit(solution)/shard_map/all_gather | solution.py:76
  780.9 16.7 multiply_convert_fusion.1
  797.7 94.8 %all-gather.36.cloned.1.call-done = bf16[4608,2304]{0,1:T(8,128)(2,1)} async-done(((bf16[4608,144]{0,1:T(8,128)(2,1)}), bf16[4608,2304]{0,1:T(8,128)(2,1)}) %all-gather.36.cloned.1.call-update) | async-done | bytes 21233680 | tf_op jit(solution)/shard_map/all_gather | solution.py:77
  892.4 12.2 fusion.107
  906.5 33.1 %reduce-scatter.15.cloned.1.call-done = f32[128,2304]{1,0:T(8,128)} async-done(((f32[256,2304]{1,0:T(8,128)}), f32[128,2304]{1,0:T(8,128)}) %reduce-scatter.15.cloned.1.call-update) | async-done | bytes 1179664 | tf_op jit(solution)/shard_map/reduce_scatter | solution.py:93
  946.6 22.9 all-gather.38.cloned.1.call-done
  969.4 14.6 multiply_convert_fusion
  984.0 13.1 fusion.108
  997.1 12.3 convolution_add_fusion
  1009.7 34.7 %reduce-scatter.17.cloned.1.call-done = f32[128,2304]{1,0:T(8,128)} async-done(((f32[256,2304]{1,0:T(8,128)}), f32[128,2304]{1,0:T(8,128)}) %reduce-scatter.17.cloned.1.call-update) | async-done | bytes 1179664 | tf_op jit(solution)/shard_map/reduce_scatter | solution.py:93
  1065.2 14.5 all-to-all-done.4
  1083.9 9.9 fusion.53
  1094.2 16.8 all_to_all.128
  1111.4 5.3 convolution_convert_fusion.4
  1117.7 9.3 fusion.47
  1132.5 45.2 %reduce-scatter.29.cloned.1.call-done = bf16[1024,2304]{1,0:T(8,128)(2,1)} async-done(((bf16[2048,2304]{1,0:T(8,128)(2,1)}), bf16[1024,2304]{1,0:T(8,128)(2,1)}) %reduce-scatter.29.cloned.1.call-update) | async-done | bytes 4718608 | tf_op jit(solution)/shard_map/reduce_scatter | solution.py:365
  1177.8 6.7 copy.175
  1184.5 106.0 %reduce-scatter.21.cloned.1.call-done = bf16[2304,1024]{1,0:T(8,128)(2,1)} async-done(((bf16[2304,2048]{1,0:T(8,128)(2,1)}), bf16[2304,1024]{1,0:T(8,128)(2,1)}) %reduce-scatter.21.cloned.1.call-update) | async-done | bytes 4718608 | tf_op jit(solution)/shard_map/reduce_scatter | solution.py:362
  1290.6 12.4 convolution_convert_fusion
  1304.3 11.7 convolution_convert_fusion.1
  1316.3 11.9 convolution_convert_fusion.2
  1329.6 7.7 all_to_all.129
  1337.4 5.2 fusion.95
  1342.9 7.6 all_to_all.130
  1355.9 7.7 fusion.109
  1370.4 41.4 %all-reduce.9 = (f32[32]{0:T(128)S(1)}, f32[2304]{0:T(1024)S(1)}, f32[2304]{0:T(1024)S(1)}, f32[2304]{0:T(1024)S(1)}, f32[2304]{0:T(1024)S(1)}) all-reduce(f32[32]{0:T(128)S(1)} %broadcast_in_dim.120, f32[2304]{0:T(1024)S(1)} %get-tuple-element.171, ...), channel_id=3, replica_groups=mesh['dp'=4,'blk'=4,'seq'=2] {'dp','blk','seq'}, use_global_device_ids=true, to_apply=%region_10.11.clone | all-reduce | flops 9248 | bytes 73984
  1419.1 64.0 %reduce-scatter.23.cloned.1.call-done = bf16[144,1024]{1,0:T(8,128)(2,1)} async-done(((bf16[2304,1024]{1,0:T(8,128)(2,1)}), bf16[144,1024]{1,0:T(8,128)(2,1)}) %reduce-scatter.23.cloned.1.call-update) | async-done | bytes 294928 | tf_op jit(solution)/shard_map/reduce_scatter | solution.py:393
  1485.0 215.1 %reduce-scatter.35.cloned.1.call-done = bf16[4608,144]{0,1:T(8,128)(2,1)} async-done(((bf16[4608,2304]{0,1:T(8,128)(2,1)}), bf16[4608,144]{0,1:T(8,128)(2,1)}) %reduce-scatter.35.cloned.1.call-update) | async-done | bytes 1327120 | tf_op jit(solution)/shard_map/reduce_scatter | solution.py:390
  1703.2 213.7 %reduce-scatter.33.cloned.1.call-done = bf16[144,4608]{1,0:T(8,128)(2,1)} async-done(((bf16[2304,4608]{1,0:T(8,128)(2,1)}), bf16[144,4608]{1,0:T(8,128)(2,1)}) %reduce-scatter.33.cloned.1.call-update) | async-done | bytes 1327120 | tf_op jit(solution)/shard_map/reduce_scatter | solution.py:387
  1919.9 213.7 %reduce-scatter.31.cloned.1.call-done = bf16[144,4608]{1,0:T(8,128)(2,1)} async-done(((bf16[2304,4608]{1,0:T(8,128)(2,1)}), bf16[144,4608]{1,0:T(8,128)(2,1)}) %reduce-scatter.31.cloned.1.call-update) | async-done | bytes 1327120 | tf_op jit(solution)/shard_map/reduce_scatter | solution.py:384
  2136.7 138.6 %reduce-scatter.27.cloned.1.call-done = f32[72,1024]{1,0:T(8,128)} async-done(((f32[2304,1024]{1,0:T(8,128)}), f32[72,1024]{1,0:T(8,128)}) %reduce-scatter.27.cloned.1.call-update) | async-done | bytes 294928 | tf_op jit(solution)/shard_map/reduce_scatter | solution.py:377
  2275.2 141.7 %reduce-scatter.25.cloned.1.call-done = f32[72,1024]{1,0:T(8,128)} async-done(((f32[2304,1024]{1,0:T(8,128)}), f32[72,1024]{1,0:T(8,128)}) %reduce-scatter.25.cloned.1.call-update) | async-done | bytes 294928 | tf_op jit(solution)/shard_map/reduce_scatter | solution.py:376
  (221 shorter events, 118.5 us)
Async XLA Ops:
  7.2 59.0 %all-gather.22.cloned.1.call-start = ((), (), s32[]{:S(2)}) async-start(), calls=%async_computation.24 | async-start | bytes 5013504 | tf_op jit(solution)/shard_map/all_gather | solution.py:78
  7.9 58.3 %copy-start.32 = (bf16[72]{0:T(256)(128)(2,1)S(1)}, bf16[72]{0:T(256)(128)(2,1)}, u32[]{:S(2)}) copy-start(bf16[72]{0:T(256)(128)(2,1)} %param.25) | copy-start | bytes 436
  7.9 58.6 %copy-start.33 = (bf16[72]{0:T(256)(128)(2,1)S(1)}, bf16[72]{0:T(256)(128)(2,1)}, u32[]{:S(2)}) copy-start(bf16[72]{0:T(256)(128)(2,1)} %param.24) | copy-start | bytes 436
  7.9 58.8 %copy-start.34 = (bf16[72]{0:T(256)(128)(2,1)S(1)}, bf16[72]{0:T(256)(128)(2,1)}, u32[]{:S(2)}) copy-start(bf16[72]{0:T(256)(128)(2,1)} %param.19) | copy-start | bytes 436
  7.9 59.1 %copy-start.35 = (bf16[72]{0:T(256)(128)(2,1)S(1)}, bf16[72]{0:T(256)(128)(2,1)}, u32[]{:S(2)}) copy-start(bf16[72]{0:T(256)(128)(2,1)} %param.29) | copy-start | bytes 436
  8.0 123.3 %all-gather.18.cloned.1.call-start = ((), (), s32[]{:S(2)}) async-start(), calls=%async_computation.22 | async-start | bytes 4866048 | tf_op jit(solution)/shard_map/all_gather | solution.py:68
  8.7 98.4 %copy-start = (bf16[128,2304]{1,0:T(8,128)(2,1)S(1)}, bf16[128,2304]{1,0:T(8,128)(2,1)}, u32[]{:S(2)}) copy-start(bf16[128,2304]{1,0:T(8,128)(2,1)} %param.15) | copy-start | bytes 1769476
  8.7 187.4 %all-gather.14.cloned.1.call-start = ((), (), s32[]{:S(2)}) async-start(), calls=%async_computation.20 | async-start | bytes 4866048 | tf_op jit(solution)/shard_map/all_gather | solution.py:69
  9.4 240.3 %all-gather.26.cloned.1.call-start = ((), (), s32[]{:S(2)}) async-start(), calls=%async_computation.26 | async-start | bytes 5013504 | tf_op jit(solution)/shard_map/all_gather | solution.py:79
  10.0 357.7 %all-gather.24.cloned.1.call-start = ((), (), s32[]{:S(2)}) async-start(), calls=%async_computation.25 | async-start | bytes 14155776 | tf_op jit(solution)/shard_map/all_gather | solution.py:82
  66.2 320.3 %all-gather.20.cloned.1.call-start = ((), (), s32[]{:S(2)}) async-start(), calls=%async_computation.23 | async-start | bytes 1310720 | tf_op jit(solution)/shard_map/all_gather | solution.py:197
  143.5 261.9 %all-gather.16.cloned.1.call-start = ((), (), s32[]{:S(2)}) async-start(), calls=%async_computation.21 | async-start | bytes 1310720 | tf_op jit(solution)/shard_map/all_gather | solution.py:198
  207.8 42.0 %copy-start.29 = (s32[4,8]{1,0:T(4,128)S(1)}, s32[4,8]{1,0:T(4,128)}, u32[]{:S(2)}) copy-start(s32[4,8]{1,0:T(4,128)} %param.18) | copy-start | bytes 388
  208.7 316.3 %all-gather.28.cloned.1.call-start = ((), (), s32[]{:S(2)}) async-start(), calls=%async_computation.27 | async-start | bytes 14155776 | tf_op jit(solution)/shard_map/all_gather | solution.py:83
  373.7 11.6 all-to-all-start.2
  378.1 27.3 %copy-start.13 = (pred[256,1024]{0,1:T(8,128)(4,1)}, pred[256,1024]{0,1:T(8,128)(4,1)S(1)}, u32[]{:S(2)}) copy-start(pred[256,1024]{0,1:T(8,128)(4,1)S(1)} %fusion.70) | copy-start | bytes 786436
  388.8 20.9 copy-start.20
  392.2 17.6 copy-start.22
  410.8 12.2 all-to-all-start.3
  414.4 143.5 %all-gather.30.cloned.1.call-start = ((), (), s32[]{:S(2)}) async-start(), calls=%async_computation.28 | async-start | bytes 1769472 | tf_op jit(solution)/shard_map/all_gather | solution.py:89
  533.9 510.5 %copy-start.26 = (f32[128]{0:T(128)}, f32[128]{0:T(128)S(1)}, u32[]{:S(2)}) copy-start(f32[128]{0:T(128)S(1)} %get-tuple-element.199) | copy-start | bytes 1540
  534.9 134.4 %all-gather.32.cloned.1.call-start = ((), (), s32[]{:S(2)}) async-start(), calls=%async_computation.29 | async-start | bytes 22560768 | tf_op jit(solution)/shard_map/all_gather | solution.py:75
  535.5 245.4 %all-gather.34.cloned.1.call-start = ((), (), s32[]{:S(2)}) async-start(), calls=%async_computation.30 | async-start | bytes 22560768 | tf_op jit(solution)/shard_map/all_gather | solution.py:76
  536.3 356.2 %all-gather.36.cloned.1.call-start = ((), (), s32[]{:S(2)}) async-start(), calls=%async_computation.31 | async-start | bytes 22560768 | tf_op jit(solution)/shard_map/all_gather | solution.py:77
  536.8 402.7 %reduce-scatter.15.cloned.1.call-start = ((), (), s32[]{:S(2)}) async-start(), calls=%async_computation.32 | async-start | bytes 3538944 | tf_op jit(solution)/shard_map/reduce_scatter | solution.py:93
  557.8 223.1 %copy-start.6 = (bf16[256,2304]{1,0:T(8,128)(2,1)S(1)}, bf16[256,2304]{1,0:T(8,128)(2,1)}, u32[]{:S(2)}) copy-start(bf16[256,2304]{1,0:T(8,128)(2,1)} %all-gather.30.cloned.1.call-done) | copy-start | bytes 3538948
  892.4 12.7 copy-start.19
  904.6 64.8 %all-gather.38.cloned.1.call-start = ((), (), s32[]{:S(2)}) async-start(), calls=%async_computation.33 | async-start | bytes 1769472 | tf_op jit(solution)/shard_map/all_gather | solution.py:89
  906.5 40.0 %copy-start.27 = (pred[128]{0:T(512)(128)(4,1)}, pred[128]{0:T(512)(128)(4,1)S(1)}, u32[]{:S(2)}) copy-start(pred[128]{0:T(512)(128)(4,1)S(1)} %dynamic_slice.33) | copy-start | bytes 388
  946.5 97.9 %reduce-scatter.17.cloned.1.call-start = ((), (), s32[]{:S(2)}) async-start(), calls=%async_computation.34 | async-start | bytes 3538944 | tf_op jit(solution)/shard_map/reduce_scatter | solution.py:93
  984.0 13.2 copy-start.10
  984.0 13.1 copy-start.11
  1009.5 36.7 %copy-start.25 = (f32[128]{0:T(128)S(1)}, f32[128]{0:T(128)}, u32[]{:S(2)}) copy-start(f32[128]{0:T(128)} %copy-done.24) | copy-start | bytes 1540
  1009.5 168.2 %reduce-scatter.29.cloned.1.call-start = ((), (), s32[]{:S(2)}) async-start(), calls=%async_computation.40 | async-start | bytes 14155776 | tf_op jit(solution)/shard_map/reduce_scatter | solution.py:365
  1055.7 9.5 copy-start.21
  1061.6 18.1 all-to-all-start.4
  1065.1 225.4 %reduce-scatter.21.cloned.1.call-start = ((), (), s32[]{:S(2)}) async-start(), calls=%async_computation.36 | async-start | bytes 14155776 | tf_op jit(solution)/shard_map/reduce_scatter | solution.py:362
  1116.6 211.7 %reduce-scatter.19.cloned.1.call-start = ((), (), s32[]{:S(2)}) async-start(), calls=%async_computation.35 | async-start | bytes 2621440 | tf_op jit(solution)/shard_map/reduce_scatter | solution.py:339
  1132.5 284.5 %reduce-scatter.37.cloned.1.call-start = ((), (), s32[]{:S(2)}) async-start(), calls=%async_computation.44 | async-start | bytes 5013504
  1184.5 106.1 %copy-start.12 = (bf16[256,2304]{1,0:T(8,128)(2,1)S(1)}, bf16[256,2304]{1,0:T(8,128)(2,1)}, u32[]{:S(2)}) copy-start(bf16[256,2304]{1,0:T(8,128)(2,1)} %all-gather.38.cloned.1.call-done) | copy-start | bytes 3538948
  1184.5 298.7 %reduce-scatter.23.cloned.1.call-start = ((), (), s32[]{:S(2)}) async-start(), calls=%async_computation.37 | async-start | bytes 5013504 | tf_op jit(solution)/shard_map/reduce_scatter | solution.py:393
  1290.5 409.5 %reduce-scatter.35.cloned.1.call-start = ((), (), s32[]{:S(2)}) async-start(), calls=%async_computation.43 | async-start | bytes 22560768 | tf_op jit(solution)/shard_map/reduce_scatter | solution.py:390
  1303.1 613.8 %reduce-scatter.33.cloned.1.call-start = ((), (), s32[]{:S(2)}) async-start(), calls=%async_computation.42 | async-start | bytes 22560768 | tf_op jit(solution)/shard_map/reduce_scatter | solution.py:387
  1316.0 817.5 %reduce-scatter.31.cloned.1.call-start = ((), (), s32[]{:S(2)}) async-start(), calls=%async_computation.41 | async-start | bytes 22560768 | tf_op jit(solution)/shard_map/reduce_scatter | solution.py:384
  1328.2 947.0 %reduce-scatter.27.cloned.1.call-start = ((), (), s32[]{:S(2)}) async-start(), calls=%async_computation.39 | async-start | bytes 9732096 | tf_op jit(solution)/shard_map/reduce_scatter | solution.py:377
  1342.7 1074.2 %reduce-scatter.25.cloned.1.call-start = ((), (), s32[]{:S(2)}) async-start(), calls=%async_computation.38 | async-start | bytes 9732096 | tf_op jit(solution)/shard_map/reduce_scatter | solution.py:376
  1365.4 50.0 %copy-start.5 = (f32[128,2304]{1,0:T(8,128)S(1)}, f32[128,2304]{1,0:T(8,128)}, u32[]{:S(2)}) copy-start(f32[128,2304]{1,0:T(8,128)} %copy-done.4) | copy-start | bytes 3538948
  1365.4 50.0 %copy-start.30 = (f32[128]{0:T(128)S(1)}, f32[128]{0:T(128)}, u32[]{:S(2)}) copy-start(f32[128]{0:T(128)} %get-tuple-element.194) | copy-start | bytes 1540
  (18 other events, 67.9 us)
Sparse Core Ops, SparseCore 0:
  10.3 55.8 all-gather.21
  69.1 62.1 all-gather.17
  134.2 61.9 all-gather.13
  198.3 51.4 all-gather.25
  251.2 116.5 all-gather.23
  369.7 16.6 all-gather.19
  388.6 16.8 all-gather.15
  407.0 117.9 all-gather.27
  535.0 22.7 all-gather.29
  559.3 109.9 all-gather.31
  670.9 109.9 all-gather.33
  782.4 110.0 all-gather.35
  904.8 34.7 reduce-scatter.14
  946.6 22.7 all-gather.37
  1009.6 34.7 reduce-scatter.16
  1055.8 121.9 reduce-scatter.28
  1179.9 110.5 reduce-scatter.20
  1293.5 31.1 reduce-scatter.18
  1328.5 75.8 reduce-scatter.36
  1408.1 74.9 reduce-scatter.22
  1487.3 212.7 reduce-scatter.34
  1704.2 212.5 reduce-scatter.32
  1920.9 212.5 reduce-scatter.30
  2139.9 135.2 reduce-scatter.26
  2281.7 135.1 reduce-scatter.24
where the time goes:
time: 2430 us
  waiting for transfers between devices  2000 us (82%)
  matrix products  209 us (9%)
  blocking collectives  130 us (5%)
  other arithmetic  32.5 us (1%)
  local copies, waits for them, and re-layouts  26.5 us (1%)
    reduce_scatter x1, waiting for transfers between devices, shards(): lax.psum_scatter(grad_down_local.astype(jnp.bfloat16), ('dp', 'blk'), sca...  215 us
    reduce_scatter x1, waiting for transfers between devices, shards(): lax.psum_scatter(grad_gate_local.astype(jnp.bfloat16), ('dp', 'blk'), sca...  214 us
    reduce_scatter x1, waiting for transfers between devices, shards(): lax.psum_scatter(grad_up_local.astype(jnp.bfloat16), ('dp', 'blk'), scatt...  214 us
    reduce_scatter x1, waiting for transfers between devices, shards(): lax.psum_scatter(grad_key_local, ('dp', 'blk', 'seq'), scatter_dimension=...  142 us
    reduce_scatter x1, waiting for transfers between devices, shards(): lax.psum_scatter(grad_value_local, ('dp', 'blk', 'seq'), scatter_dimensio...  139 us
    all_gather x1, waiting for transfers between devices, fetch_weights(): lax.all_gather(feed_set[3], 'seq', axis=1, tiled=True)  118 us
    all_gather x1, waiting for transfers between devices, fetch_weights(): lax.all_gather(gate_weight, ('dp', 'blk'), axis=0, tiled=True)  111 us
    reduce_scatter x1, waiting for transfers between devices, shards(): lax.psum_scatter(grad_query_local.astype(jnp.bfloat16), 'seq', scatter_di...  106 us
  transfers between devices with their start and end apart: 28, of which 26 were waited for; matrix products, arithmetic and copies ran while one was open for 8% of the time, Pallas kernels for 0%

commit v1 on v0

v1 whole, which is shorter than its diff:
```python
import jax
import jax.numpy as jnp
from jax import lax
from jax.sharding import PartitionSpec as P

HQ = 8
KVH = 4
HD = 256


EPS = 1e-06
CAP = 50.0
SCALE = 0.0625
NEG = -1e30


def segment_ids(lengths, total_rows):
    ends_at = jnp.cumsum(lengths)
    places = jnp.arange(total_rows, dtype=jnp.int32)
    number = jnp.sum((places[:, None] >= ends_at[None, :]).astype(jnp.int32), axis=1)
    return jnp.where(number == lengths.shape[0] - 1, -1, number)


def scale_rows(source, gain):
    inverse = lax.rsqrt(jnp.mean(source * source, axis=-1, keepdims=True) + EPS)
    return (source * inverse * gain, inverse)


def scale_back(source, inverse, gain, upstream):
    weighted = upstream * gain
    inner_mean = jnp.mean(weighted * source, axis=-1, keepdims=True)
    grad_source = inverse * weighted - source * (inverse * inverse * inverse) * inner_mean
    grad_gain = jnp.sum(upstream * source * inverse, axis=0)
    return (grad_source, grad_gain)


def inner_rows(left_side, right_side):
    return lax.dot_general(
        left_side, right_side, (((0,), (0,)), ((), ())), preferred_element_type=jnp.float32
    )


def against(left_side, right_side):
    return lax.dot_general(
        left_side, right_side, (((1,), (1,)), ((), ())), preferred_element_type=jnp.float32
    )


def geglu(gate_value, up_value):
    return jax.nn.gelu(gate_value, approximate=True) * up_value


def swap_pairs(size):
    return [(place, size - 1 - place) for place in range(size)]


def pair_gather(rows_here):
    if lax.axis_size("seq") != 2:
        return lax.all_gather(rows_here, "seq", axis=0, tiled=True)
    return jnp.concatenate([rows_here, lax.ppermute(rows_here, "seq", swap_pairs(2))], axis=0)


def pair_sum(partial):
    if lax.axis_size("seq") != 2:
        return lax.psum_scatter(
            partial.astype(jnp.bfloat16), "seq", scatter_dimension=0, tiled=True
        ).astype(jnp.float32)
    half = partial.shape[0] // 2
    arrived = lax.ppermute(partial[half:].astype(jnp.bfloat16), "seq", swap_pairs(2))
    return partial[:half] + arrived.astype(jnp.float32)


def pair_places(own_rows, seq_index, seq_size):
    if seq_size != 2:
        return jnp.arange(own_rows * seq_size, dtype=jnp.int32)
    here = jnp.arange(own_rows, dtype=jnp.int32)
    return jnp.concatenate([seq_index * own_rows + here, (1 - seq_index) * own_rows + here])


def seg_at(lengths, places):
    ends_at = jnp.cumsum(lengths)
    number = jnp.sum((places[:, None] >= ends_at[None, :]).astype(jnp.int32), axis=1)
    return jnp.where(number == lengths.shape[0] - 1, -1, number)


def columns_to_planes(matrix):
    planes = lax.axis_size("dp")
    rows, columns = matrix.shape
    return matrix.reshape(rows, planes, columns // planes).transpose(1, 0, 2)


def to_feed_order(rows_natural):
    planes, cycle = lax.axis_size("dp"), lax.axis_size("blk")
    rows, width = rows_natural.shape
    share = width // (planes * cycle)
    return (
        rows_natural.reshape(rows, planes, cycle, share).transpose(0, 2, 1, 3).reshape(rows, width)
    )


def from_feed_order(rows_feed):
    planes, cycle = lax.axis_size("dp"), lax.axis_size("blk")
    rows, width = rows_feed.shape
    share = width // (planes * cycle)
    return rows_feed.reshape(rows, cycle, planes, share).transpose(0, 2, 1, 3).reshape(rows, width)


def shards(
    inputs,
    teacher,
    valid_mask,
    doc_lengths,
    gain_pre_attention,
    query_weight,
    key_weight,
    value_weight,
    output_weight,
    gain_post_attention,
    gain_pre_feed,
    gate_weight,
    up_weight,
    down_weight,
    gain_post_feed,
):
    seq_size = lax.axis_size("seq")
    cycle_size = lax.axis_size("blk")
    planes = lax.axis_size("dp")
    own_rows = inputs.shape[0]
    width = inputs.shape[1]
    share = width // (planes * cycle_size)
    block_rows = own_rows * seq_size
    seq_length = block_rows * cycle_size
    heads_here = HQ // seq_size
    kv_total = max(KVH, seq_size)
    repeats = kv_total // KVH
    kv_here = kv_total // seq_size
    group_size = heads_here // kv_here
    cycle_index = lax.axis_index("blk")
    seq_index = lax.axis_index("seq")
    data_index = lax.axis_index("dp")
    seg_every = jax.vmap(lambda row_lengths: segment_ids(row_lengths, seq_length))(doc_lengths)
    live_every = ((valid_mask.reshape(seg_every.shape) == 1) & (seg_every >= 0)).reshape(-1)
    count = jnp.maximum(jnp.sum(live_every.astype(jnp.float32)), 1.0)
    token_total = float(seg_every.size)
    own_lengths = lax.dynamic_index_in_dim(doc_lengths, data_index, 0, keepdims=False)
    block_first = cycle_index * block_rows
    own_first = block_first + seq_index * own_rows
    live_own = lax.dynamic_slice_in_dim(live_every, data_index * seq_length + own_first, own_rows)
    in_block = pair_places(own_rows, seq_index, seq_size)
    positions = block_first + in_block
    key_places = (
        jnp.arange(cycle_size, dtype=jnp.int32)[:, None] * block_rows + in_block[None, :]
    ).reshape(-1)
    seg_block = seg_at(own_lengths, positions)
    seg_all = seg_at(own_lengths, key_places)

    gains = lax.all_gather(
        jnp.stack([gain_pre_attention, gain_post_attention, gain_pre_feed, gain_post_feed]),
        ("dp", "blk", "seq"),
        axis=0,
        tiled=False,
    )
    gains = gains.transpose(1, 0, 2).reshape(4, width).astype(jnp.float32)
    gain_first, gain_second, gain_third, gain_fourth = gains[0], gains[1], gains[2], gains[3]
    spread = max(1, seq_size // KVH)
    if seq_size <= KVH:
        kv_both = jnp.concatenate(
            [
                key_weight.reshape(-1, seq_size, KVH * HD // seq_size),
                value_weight.reshape(-1, seq_size, KVH * HD // seq_size),
            ],
            axis=2,
        ).transpose(1, 0, 2)
    else:
        kv_both = jnp.repeat(
            jnp.concatenate(
                [key_weight.reshape(-1, KVH, HD), value_weight.reshape(-1, KVH, HD)], axis=2
            ).transpose(1, 0, 2),
            spread,
            axis=0,
        )
    kv_mine = lax.all_to_all(kv_both, "seq", split_axis=0, concat_axis=0, tiled=True).reshape(
        share, 2 * kv_here * HD
    )
    project_local = jnp.concatenate([query_weight, kv_mine], axis=1)
    project_weight = lax.all_gather(project_local, ("dp", "blk"), axis=0, tiled=True)
    output_across = lax.all_gather(output_weight.T, ("dp", "blk"), axis=0, tiled=True)
    feed_local = jnp.concatenate(
        [
            columns_to_planes(gate_weight),
            columns_to_planes(up_weight),
            columns_to_planes(down_weight.T),
        ],
        axis=2,
    )
    feed_plane = lax.all_to_all(feed_local, "dp", split_axis=0, concat_axis=0, tiled=True)
    units = feed_plane.shape[2] // 3
    feed_weight = lax.all_gather(
        feed_plane.reshape(planes * share, 3 * units), "blk", axis=0, tiled=True
    )
    gate_matrix = feed_weight[:, :units]
    up_matrix = feed_weight[:, units : 2 * units]
    down_across = feed_weight[:, 2 * units :]

    source = inputs.astype(jnp.float32)
    normed_attention, inverse_one = scale_rows(source, gain_first)
    attention_in = normed_attention.astype(jnp.bfloat16)
    block_in = pair_gather(attention_in)
    projected = jnp.dot(block_in, project_weight, preferred_element_type=jnp.float32).astype(
        jnp.bfloat16
    )
    queries_group = projected[:, : heads_here * HD].reshape(block_rows, kv_here, group_size, HD)
    kv_block = projected[:, heads_here * HD :].reshape(block_rows, 2, kv_here, HD)
    kv_all = lax.all_gather(kv_block, "blk", axis=0, tiled=True)
    keys_all, values_all = kv_all[:, 0], kv_all[:, 1]

    raw_scores = (
        jnp.einsum("qgjd,kgd->gjqk", queries_group, keys_all, preferred_element_type=jnp.float32)
        * SCALE
    )
    capped = CAP * jnp.tanh(raw_scores / CAP)
    allowed = (
        (key_places[None, :] <= positions[:, None])
        & (seg_all[None, :] == seg_block[:, None])
        & ((seg_all[None, :] >= 0) | (key_places[None, :] == positions[:, None]))
    )[None, None]
    masked = jnp.where(allowed, capped, NEG)
    highest = jnp.max(masked, axis=-1, keepdims=True)
    weights = jnp.where(allowed, jnp.exp(masked - highest), 0.0)
    totals = jnp.sum(weights, axis=-1, keepdims=True)
    probs = (weights / totals).astype(jnp.bfloat16)
    log_totals = highest + jnp.log(totals)
    mixed = (
        jnp.einsum("gjqk,kgd->qgjd", probs, values_all, preferred_element_type=jnp.float32)
        .astype(jnp.bfloat16)
        .reshape(block_rows, heads_here * HD)
    )
    branch_attention = pair_sum(against(mixed, output_across))
    normed_branch, inverse_two = scale_rows(branch_attention, gain_second)
    hidden_state = source + normed_branch
    normed_feed, inverse_three = scale_rows(hidden_state, gain_third)
    feed_in = to_feed_order(normed_feed.astype(jnp.bfloat16))
    feed_rows = lax.all_gather(feed_in, ("dp", "seq"), axis=0, tiled=True)
    gate_value = jnp.dot(feed_rows, gate_matrix, preferred_element_type=jnp.float32)
    up_value = jnp.dot(feed_rows, up_matrix, preferred_element_type=jnp.float32)
    product_rows = geglu(gate_value, up_value).astype(jnp.bfloat16)
    branch_feed = from_feed_order(
        lax.psum_scatter(
            against(product_rows, down_across).astype(jnp.bfloat16),
            ("dp", "seq"),
            scatter_dimension=0,
            tiled=True,
        )
    ).astype(jnp.float32)
    normed_out, inverse_four = scale_rows(branch_feed, gain_fourth)
    layer_rows = hidden_state + normed_out
    difference = jnp.where(live_own[:, None], layer_rows - teacher.astype(jnp.float32), 0.0)
    error_own = jnp.sum(difference * difference)
    upstream = difference * (2.0 * token_total / count)

    grad_branch_feed, grad_gain_four = scale_back(branch_feed, inverse_four, gain_fourth, upstream)
    feed_grad_rows = lax.all_gather(
        to_feed_order(grad_branch_feed.astype(jnp.bfloat16)), ("dp", "seq"), axis=0, tiled=True
    )
    grad_product = jnp.dot(feed_grad_rows, down_across, preferred_element_type=jnp.float32)
    geglu_value, geglu_pull = jax.vjp(geglu, gate_value, up_value)
    grad_gate_value, grad_up_value = geglu_pull(grad_product)
    gate_back = grad_gate_value.astype(jnp.bfloat16)
    up_back = grad_up_value.astype(jnp.bfloat16)
    grad_feed_in = from_feed_order(
        lax.psum_scatter(
            (against(gate_back, gate_matrix) + against(up_back, up_matrix)).astype(jnp.bfloat16),
            ("dp", "seq"),
            scatter_dimension=0,
            tiled=True,
        )
    ).astype(jnp.float32)
    feed_grads = jnp.concatenate(
        [
            inner_rows(feed_rows, gate_back).astype(jnp.bfloat16),
            inner_rows(feed_rows, up_back).astype(jnp.bfloat16),
            inner_rows(feed_grad_rows, product_rows).astype(jnp.bfloat16),
        ],
        axis=1,
    )
    feed_plane_grads = lax.psum_scatter(feed_grads, "blk", scatter_dimension=0, tiled=True)
    feed_own_grads = lax.all_to_all(
        feed_plane_grads.reshape(planes, share, 3 * units),
        "dp",
        split_axis=0,
        concat_axis=0,
        tiled=True,
    ).astype(jnp.float32)

    def from_planes(part):
        return part.transpose(1, 0, 2).reshape(share, planes * units)

    gate_gradient = from_planes(feed_own_grads[:, :, :units])
    up_gradient = from_planes(feed_own_grads[:, :, units : 2 * units])
    down_gradient = from_planes(feed_own_grads[:, :, 2 * units :]).T

    grad_hidden_part, grad_gain_three = scale_back(
        hidden_state, inverse_three, gain_third, grad_feed_in
    )
    grad_hidden = upstream + grad_hidden_part
    grad_branch_attention, grad_gain_two = scale_back(
        branch_attention, inverse_two, gain_second, grad_hidden
    )
    branch_back = pair_gather(grad_branch_attention.astype(jnp.bfloat16))
    mixed_back = jnp.dot(branch_back, output_across, preferred_element_type=jnp.float32).astype(
        jnp.bfloat16
    )
    output_gradient = lax.psum_scatter(
        inner_rows(branch_back, mixed).astype(jnp.bfloat16),
        ("dp", "blk"),
        scatter_dimension=0,
        tiled=True,
    )
    mixed_group = mixed_back.reshape(block_rows, kv_here, group_size, HD)
    back_probs = jnp.where(allowed, jnp.exp(capped - log_totals), 0.0)
    grad_probs = jnp.einsum(
        "qgjd,kgd->gjqk", mixed_group, values_all, preferred_element_type=jnp.float32
    )
    centre = jnp.sum(back_probs * grad_probs, axis=-1, keepdims=True)
    score_back = (
        back_probs * (grad_probs - centre) * (1.0 - capped / CAP * (capped / CAP))
    ).astype(jnp.bfloat16)
    query_back = (
        (
            jnp.einsum("gjqk,kgd->qgjd", score_back, keys_all, preferred_element_type=jnp.float32)
            * SCALE
        )
        .astype(jnp.bfloat16)
        .reshape(block_rows, heads_here * HD)
    )
    grad_keys = (
        jnp.einsum("gjqk,qgjd->kgd", score_back, queries_group, preferred_element_type=jnp.float32)
        * SCALE
    )
    grad_values = jnp.einsum(
        "gjqk,qgjd->kgd",
        back_probs.astype(jnp.bfloat16),
        mixed_group,
        preferred_element_type=jnp.float32,
    )
    kv_back = lax.psum_scatter(
        jnp.stack([grad_keys, grad_values], axis=1).astype(jnp.bfloat16),
        "blk",
        scatter_dimension=0,
        tiled=True,
    ).reshape(block_rows, 2 * kv_here * HD)
    projected_back = jnp.concatenate([query_back, kv_back], axis=1)
    attention_back = pair_sum(against(projected_back, project_weight))
    project_gradient = lax.psum_scatter(
        inner_rows(block_in, projected_back).astype(jnp.bfloat16),
        ("dp", "blk"),
        scatter_dimension=0,
        tiled=True,
    )
    query_gradient = project_gradient[:, : heads_here * HD].astype(jnp.float32)
    kv_gradient = lax.all_to_all(
        project_gradient[:, heads_here * HD :].reshape(seq_size, share // seq_size, -1),
        "seq",
        split_axis=0,
        concat_axis=0,
        tiled=True,
    ).astype(jnp.float32)
    kv_gradient = jnp.sum(
        kv_gradient.reshape(
            seq_size // spread, spread, share // seq_size, 2, kv_total // seq_size * HD
        ),
        axis=1,
    ).transpose(2, 1, 0, 3).reshape(2, share // seq_size, KVH * HD)

    grad_source, grad_gain_one = scale_back(source, inverse_one, gain_first, attention_back)
    inputs_gradient = grad_hidden + grad_source
    pieces = jnp.concatenate(
        [
            jnp.stack([grad_gain_one, grad_gain_two, grad_gain_three, grad_gain_four]),
            jnp.full((4, 128), error_own, jnp.float32),
        ],
        axis=1,
    )
    summed = lax.psum(pieces, ("dp", "blk", "seq"))
    device_index = (data_index * cycle_size + cycle_index) * seq_size + seq_index
    gain_share = width // (planes * cycle_size * seq_size)
    gain_gradients = lax.dynamic_slice_in_dim(summed, device_index * gain_share, gain_share, axis=1)
    loss_value = summed[0, width] / (width * count)
    layer_output = layer_rows.astype(jnp.bfloat16)
    return (
        layer_output,
        loss_value,
        inputs_gradient,
        gain_gradients[0],
        query_gradient,
        kv_gradient[0],
        kv_gradient[1],
        output_gradient.astype(jnp.float32).T,
        gain_gradients[1],
        gain_gradients[2],
        gate_gradient,
        up_gradient,
        down_gradient,
        gain_gradients[3],
    )


def solution(mesh):
    in_specs = (
        P(("dp", "blk", "seq"), None),
        P(("dp", "blk", "seq"), None),
        P(),
        P(),
        P(("dp", "blk", "seq")),
        P(("dp", "blk"), "seq"),
        P(("dp", "blk", "seq"), None),
        P(("dp", "blk", "seq"), None),
        P("seq", ("dp", "blk")),
        P(("dp", "blk", "seq")),
        P(("dp", "blk", "seq")),
        P(("dp", "blk"), "seq"),
        P(("dp", "blk"), "seq"),
        P("seq", ("dp", "blk")),
        P(("dp", "blk", "seq")),
    )
    out_specs = (
        P(("dp", "blk", "seq"), None),
        P(),
        P(("dp", "blk", "seq"), None),
        P(("dp", "blk", "seq")),
        P(("dp", "blk"), "seq"),
        P(("dp", "blk", "seq"), None),
        P(("dp", "blk", "seq"), None),
        P("seq", ("dp", "blk")),
        P(("dp", "blk", "seq")),
        P(("dp", "blk", "seq")),
        P(("dp", "blk"), "seq"),
        P(("dp", "blk"), "seq"),
        P("seq", ("dp", "blk")),
        P(("dp", "blk", "seq")),
    )
    return jax.shard_map(shards, mesh=mesh, in_specs=in_specs, out_specs=out_specs, check_vma=False)
```

time: 2430 us -> 1310 us (0.54)
  waiting for transfers between devices: 2000 us -> 653 us
  blocking collectives: 130 us -> 339 us
  matrix products: 209 us -> 152 us
  local copies, waits for them, and re-layouts: 26.5 us -> 64.3 us
  other arithmetic: 32.5 us -> 65.4 us
    reduce_scatter x11 -> x6, waiting for transfers between devices: 1210 us -> 357 us  [the longest x1 112 us: shards(): lax.psum_scatter(feed_grads, 'blk', scatter_dimension=0, tiled=True)]
    all_gather x13 -> x6, waiting for transfers between devices: 757 us -> 243 us  [the longest x1 98.7 us: shards(): lax.all_gather(feed_plane.reshape(planes * share, 3 * units), 'blk', axis...]
    psum x0 -> x1, blocking collectives: none -> 111 us  [shards(): summed = lax.psum(pieces, ('dp', 'blk', 'seq'))]
    all_to_all x5 -> x3, blocking collectives: 48.6 us -> 159 us  [the longest x1 142 us: shards(): lax.all_to_all(feed_local, 'dp', split_axis=0, concat_axis=0, tiled=True)]
    unnamed x2 -> x0, blocking collectives: 81.2 us -> none
    all_gather x0 -> x1, blocking collectives: none -> 68.6 us  [shards(): lax.all_gather(jnp.stack([gain_pre_attention, gain_post_attention, gain_p...]
    ppermute x0 -> x4, waiting for transfers between devices: none -> 52.7 us  [the longest x2 27.2 us: pair_sum(): lax.ppermute(partial[half:].astype(jnp.bfloat16), 'seq', swap_pairs(2))]
    all_to_all x3 -> x1, waiting for transfers between devices: 30 us -> 0.01 us  [shards(): lax.all_to_all(feed_plane_grads.reshape(planes, share, 3 * units), 'dp',...]
  transfers between devices with their start and end apart: 28 -> 17, of which waited for: 26 -> 13; matrix products, arithmetic and copies ran while one was open for 8% -> 10% of each run, Pallas kernels for 0% -> 0%
where the time goes in v1:
time: 1310 us; the launch traced here: 1300 us
  waiting for transfers between devices  653 us (50%)
  blocking collectives  339 us (26%)
  matrix products  152 us (12%)
  other arithmetic  65.4 us (5%)
  local copies, waits for them, and re-layouts  64.3 us (5%)
  between operations  18.1 us (1%)
    all_to_all x1, blocking collectives, shards(): lax.all_to_all(feed_local, 'dp', split_axis=0, concat_axis=0, tiled=True)  142 us
    reduce_scatter x1, waiting for transfers between devices, shards(): lax.psum_scatter(feed_grads, 'blk', scatter_dimension=0, tiled=True)  112 us
    psum x1, blocking collectives, shards(): summed = lax.psum(pieces, ('dp', 'blk', 'seq'))  111 us
    all_gather x1, waiting for transfers between devices, shards(): lax.all_gather(feed_plane.reshape(planes * share, 3 * units), 'blk', axis...  98.7 us
    reduce_scatter x1, waiting for transfers between devices, shards(): lax.psum_scatter((against(gate_back, gate_matrix) + against(up_back, up_m...  93.8 us
    reduce_scatter x1, waiting for transfers between devices, shards(): lax.psum_scatter(against(product_rows, down_across).astype(jnp.bfloat16),...  92.9 us
    all_gather x1, waiting for transfers between devices, shards(): lax.all_gather(to_feed_order(grad_branch_feed.astype(jnp.bfloat16)), ('dp...  79.9 us
    all_gather x1, blocking collectives, shards(): lax.all_gather(jnp.stack([gain_pre_attention, gain_post_attention, gain_p...  68.6 us
  transfers between devices with their start and end apart: 17, of which 13 were waited for; matrix products, arithmetic and copies ran while one was open for 10% of the time, Pallas kernels for 0%

profile of v1, /device:TPU:0, one launch (start us, length us, event | category | flops | bytes accessed | tf_op | source)
XLA Modules:
  0.0 1303.2 jit_solution(192250695807596514)
XLA Ops:
  9.6 9.6 all_to_all.20
  21.8 68.6 %all-gather.1 = bf16[32,4,72]{2,1,0:T(4,128)(2,1)S(1)} all-gather(bf16[1,4,72]{2,1,0:T(4,128)(2,1)S(1)} %maximum_bitcast_fusion.1), channel_id=2, replica_groups=mesh['dp'=4,'blk'=4,'seq'=2] {'dp','blk','seq'}, dimensions={0}, use_global_device_ids=true | all-gather | bytes 19008 | tf_op jit(solution)/shard_map/all_gather | solution.py:157
  92.3 12.2 collective-permute-done
  105.3 6.3 convolution_convert_fusion.6
  115.7 16.1 %all-gather.11.cloned.1.call-done = bf16[1024,2,2,256]{3,0,2,1:T(8,128)(2,1)} async-done(((bf16[256,2,2,256]{3,0,2,1:T(8,128)(2,1)}), bf16[1024,2,2,256]{3,0,2,1:T(8,128)(2,1)}) %all-gather.11.cloned.1.call-update) | async-done | bytes 2097168 | tf_op jit(solution)/shard_map/all_gather | solution.py:214
  139.1 48.1 %all-gather.13.cloned.1.call-done = bf16[2304,1024]{1,0:T(8,128)(2,1)} async-done(((bf16[144,1024]{1,0:T(8,128)(2,1)}), bf16[2304,1024]{1,0:T(8,128)(2,1)}) %all-gather.13.cloned.1.call-update) | async-done | bytes 4718608 | tf_op jit(solution)/shard_map/all_gather | solution.py:187
  187.2 3.8 fusion.108
  194.2 13.8 %collective-permute-done.1 = bf16[128,2304]{1,0:T(8,128)(2,1)S(1)} collective-permute-done((bf16[128,2304]{1,0:T(8,128)(2,1)S(1)}, bf16[128,2304]{1,0:T(8,128)(2,1)S(1)}, u32[]{:S(2)}, u32[]{:S(2)}) %collective-permute-start.1) | collective-permute-done | bytes 589856 | tf_op jit(solution)/shard_map/ppermute | solution.py:69
  213.9 2.7 reshape.409
  216.6 3.5 reshape.408
  220.2 3.6 reshape.407
  223.7 3.6 pad_maximum_fusion.1
  227.7 141.6 %all_to_all.21 = bf16[4,144,3456]{2,1,0:T(8,128)(2,1)} all-to-all(bf16[4,144,3456]{2,1,0:T(8,128)(2,1)S(1)} %copy.177), channel_id=1, replica_groups=mesh['dp'=4,'blk'=4,'seq'=2] {'dp'}, dimensions={0} | all-to-all | bytes 7962624 | tf_op jit(solution)/shard_map/all_to_all | solution.py:196
  369.7 98.7 %all-gather.17.cloned.1.call-done = bf16[2304,3456]{1,0:T(8,128)(2,1)} async-done(((bf16[576,3456]{1,0:T(8,128)(2,1)}), bf16[2304,3456]{1,0:T(8,128)(2,1)}) %all-gather.17.cloned.1.call-update) | async-done | bytes 15925264 | tf_op jit(solution)/shard_map/all_gather | solution.py:198
  468.4 10.1 fusion.16
  478.5 9.6 multiply_convert_fusion.1
  488.1 9.7 convolution_convert_fusion.5
  500.7 92.9 %reduce-scatter.9.cloned.1.call-done = bf16[128,2304]{1,0:T(8,128)(2,1)} async-done(((bf16[1024,2304]{1,0:T(8,128)(2,1)}), bf16[128,2304]{1,0:T(8,128)(2,1)}) %reduce-scatter.9.cloned.1.call-update) | async-done | bytes 589840 | tf_op jit(solution)/shard_map/reduce_scatter | solution.py:248
  604.1 79.9 %all-gather.19.cloned.1.call-done = bf16[1024,2304]{0,1:T(8,128)(2,1)} async-done(((bf16[128,2304]{0,1:T(8,128)(2,1)}), bf16[1024,2304]{0,1:T(8,128)(2,1)}) %all-gather.19.cloned.1.call-update) | async-done | bytes 4718608 | tf_op jit(solution)/shard_map/all_gather | solution.py:262
  684.0 14.9 %multiply_convert_fusion = (bf16[1024,1152]{1,0:T(8,128)(2,1)S(1)}, bf16[1024,1152]{1,0:T(8,128)(2,1)S(1)}) fusion(f32[1024,1152]{1,0:T(8,128)} %copy-done.46, f32[1024,1152]{1,0:T(8,128)} %get-tuple-element.61, bf16[1024,2304]{0,1:T(8,128)(2,1)} %all-gather.19.cloned.1.call-done, bf16[2304,3456]{1,0:T(8,128)(2,1)} %all-gather.17.cloned.1.call-done), kind=kOutput, calls=%fused_computation.18 | convolution fusion | flops 5464129536 | bytes 24182784 | tf_op jit(solution)/shard_map/dot_general | solution.py:265
  698.9 10.5 fusion.14
  709.4 10.6 add_convert_fusion
  720.3 93.8 %reduce-scatter.11.cloned.1.call-done = bf16[128,2304]{1,0:T(8,128)(2,1)} async-done(((bf16[1024,2304]{1,0:T(8,128)(2,1)}), bf16[128,2304]{1,0:T(8,128)(2,1)}) %reduce-scatter.11.cloned.1.call-update) | async-done | bytes 589840 | tf_op jit(solution)/shard_map/reduce_scatter | solution.py:271
  819.7 4.5 multiply_reduce_fusion.4
  826.2 13.3 %collective-permute-done.2 = bf16[128,2304]{1,0:T(8,128)(2,1)S(1)} collective-permute-done((bf16[128,2304]{1,0:T(8,128)(2,1)S(1)}, bf16[128,2304]{1,0:T(8,128)(2,1)S(1)}, u32[]{:S(2)}, u32[]{:S(2)}) %collective-permute-start.2) | collective-permute-done | bytes 589856 | tf_op jit(solution)/shard_map/ppermute | solution.py:60
  840.3 3.7 convolution_convert_fusion.7
  844.3 4.8 fusion.57
  849.1 2.7 fusion.72
  851.8 9.1 fusion.56
  860.9 3.1 pad_maximum_fusion.2
  864.1 11.1 fusion.62
  875.1 20.4 %reduce-scatter.13.cloned.1.call-done = bf16[256,2,2,256]{0,3,2,1:T(8,128)(2,1)} async-done(((bf16[1024,2,2,256]{0,3,2,1:T(8,128)(2,1)}), bf16[256,2,2,256]{0,3,2,1:T(8,128)(2,1)}) %reduce-scatter.13.cloned.1.call-update) | async-done | bytes 524304 | tf_op jit(solution)/shard_map/reduce_scatter | solution.py:346
  895.5 6.3 convolution_convert_fusion.3
  902.1 9.1 convolution_convert_fusion
  911.2 9.3 convolution_convert_fusion.1
  920.5 6.4 convolution_convert_fusion.2
  927.0 23.8 %pad_maximum_fusion = bf16[2304,3456]{0,1:T(8,128)(2,1)} fusion(bf16[2304,1152]{0,1:T(8,128)(2,1)S(1)} %convolution_convert_fusion, bf16[2304,1152]{0,1:T(8,128)(2,1)S(1)} %convolution_convert_fusion.1, bf16[2304,1152]{0,1:T(8,128)(2,1)S(1)} %convolution_convert_fusion.2), kind=kLoop, calls=%fused_computation.1 | loop fusion | flops 47775744 | bytes 31850496 | tf_op jit(solution)/shard_map/concatenate | solution.py:278
  950.8 20.4 %copy.216 = bf16[2304,3456]{1,0:T(8,128)(2,1)} copy(bf16[2304,3456]{0,1:T(8,128)(2,1)} %pad_maximum_fusion) | data formatting | bytes 31850496
  972.4 3.5 convolution_convert_fusion.4
  976.0 37.2 %reduce-scatter.15.cloned.1.call-done = bf16[144,2048]{1,0:T(8,128)(2,1)} async-done(((bf16[2304,2048]{1,0:T(8,128)(2,1)}), bf16[144,2048]{1,0:T(8,128)(2,1)}) %reduce-scatter.15.cloned.1.call-update) | async-done | bytes 589840 | tf_op jit(solution)/shard_map/reduce_scatter | solution.py:354
  1015.1 8.0 all_to_all.22
  1023.1 112.4 %reduce-scatter.19.cloned.1.call-done = bf16[576,3456]{1,0:T(8,128)(2,1)} async-done(((bf16[2304,3456]{1,0:T(8,128)(2,1)}), bf16[576,3456]{1,0:T(8,128)(2,1)}) %reduce-scatter.19.cloned.1.call-update) | async-done | bytes 3981328 | tf_op jit(solution)/shard_map/reduce_scatter | solution.py:286
  1135.5 4.9 all-to-all-start.3
  1140.5 6.4 fusion.74
  1150.0 13.4 %collective-permute-done.3 = bf16[128,2304]{1,0:T(8,128)(2,1)S(1)} collective-permute-done((bf16[128,2304]{1,0:T(8,128)(2,1)S(1)}, bf16[128,2304]{1,0:T(8,128)(2,1)S(1)}, u32[]{:S(2)}, u32[]{:S(2)}) %collective-permute-start.3) | collective-permute-done | bytes 589856 | tf_op jit(solution)/shard_map/ppermute | solution.py:69
  1165.7 111.2 %psum.7 = f32[4,2432]{1,0:T(4,128)S(1)} all-reduce(f32[4,2432]{1,0:T(4,128)S(1)} %select_maximum_fusion), channel_id=1, replica_groups=mesh['dp'=4,'blk'=4,'seq'=2] {'dp','blk','seq'}, use_global_device_ids=true, to_apply=%region_24.25 | all-reduce | flops 9728 | bytes 77824 | tf_op jit(solution)/shard_map/psum | solution.py:384
  1278.7 2.8 fusion.70
  1286.2 2.7 convert_element_type.187
  (228 shorter events, 70.9 us)
Async XLA Ops:
  7.2 83.5 %copy-start = (bf16[128,2304]{1,0:T(8,128)(2,1)S(1)}, bf16[128,2304]{1,0:T(8,128)(2,1)}, u32[]{:S(2)}) copy-start(bf16[128,2304]{1,0:T(8,128)(2,1)} %param.15) | copy-start | bytes 1769476
  7.2 97.3 %all-gather.9.cloned.1.call-start = ((), (), s32[]{:S(2)}) async-start(), calls=%async_computation.10 | async-start | bytes 10027008 | tf_op jit(solution)/shard_map/all_gather | solution.py:186
  21.1 110.7 %all-gather.11.cloned.1.call-start = ((), (), s32[]{:S(2)}) async-start(), calls=%async_computation.11 | async-start | bytes 2621440 | tf_op jit(solution)/shard_map/all_gather | solution.py:214
  92.2 19.4 %copy-start.10 = (bf16[128,2304]{1,0:T(8,128)(2,1)}, bf16[128,2304]{1,0:T(8,128)(2,1)S(1)}, u32[]{:S(2)}) copy-start(bf16[128,2304]{1,0:T(8,128)(2,1)S(1)} %fusion.65) | copy-start | bytes 1769476
  92.2 12.3 collective-permute-start
  113.0 74.2 %all-gather.13.cloned.1.call-start = ((), (), s32[]{:S(2)}) async-start(), calls=%async_computation.12 | async-start | bytes 5013504 | tf_op jit(solution)/shard_map/all_gather | solution.py:187
  113.7 255.9 %all-gather.15.cloned.1.call-start = ((), (), s32[]{:S(2)}) async-start(), calls=%async_computation.13 | async-start | bytes 5308416 | tf_op jit(solution)/shard_map/all_gather | solution.py:243
  115.5 20.0 %copy-start.12 = (pred[256,1024]{0,1:T(8,128)(4,1)}, pred[256,1024]{0,1:T(8,128)(4,1)S(1)}, u32[]{:S(2)}) copy-start(pred[256,1024]{0,1:T(8,128)(4,1)S(1)} %or_and_fusion) | copy-start | bytes 786436
  115.7 18.4 %copy-start.22 = (bf16[256,1024]{0,1:T(8,128)(2,1)}, bf16[256,1024]{0,1:T(8,128)(2,1)S(1)}, u32[]{:S(2)}) copy-start(bf16[256,1024]{0,1:T(8,128)(2,1)S(1)} %copy.218) | copy-start | bytes 1572868
  139.1 48.1 %copy-start.18 = (bf16[2,256,2,256]{3,1,2,0:T(8,128)(2,1)}, bf16[2,256,2,256]{3,1,2,0:T(8,128)(2,1)S(1)}, u32[]{:S(2)}) copy-start(bf16[2,256,2,256]{3,1,2,0:T(8,128)(2,1)S(1)} %fusion.61) | copy-start | bytes 1572868
  192.5 15.5 %collective-permute-start.1 = (bf16[128,2304]{1,0:T(8,128)(2,1)S(1)}, bf16[128,2304]{1,0:T(8,128)(2,1)S(1)}, u32[]{:S(2)}, u32[]{:S(2)}) collective-permute-start(bf16[128,2304]{1,0:T(8,128)(2,1)S(1)} %slice.190), channel_id=1, source_target_pairs={{0,1},{1,0},{2,3},{3,2},{4,5},{5,4},{6,7},{7,6},{8,9},{9,8},{10,11... | collective-permute-start | bytes 1769480 | tf_op jit(solution)/shard_map/ppermute | solution.py:69
  194.2 19.6 %copy-start.28 = (f32[2304]{0:T(1024)}, f32[2304]{0:T(1024)S(1)}, u32[]{:S(2)}) copy-start(f32[2304]{0:T(1024)S(1)} %mul.468) | copy-start | bytes 27652
  210.3 6.4 copy-start.37
  212.5 7.7 copy-start.39
  213.9 254.5 %all-gather.17.cloned.1.call-start = ((), (), s32[]{:S(2)}) async-start(), calls=%async_computation.14 | async-start | bytes 19906560 | tf_op jit(solution)/shard_map/all_gather | solution.py:198
  369.3 224.2 %reduce-scatter.9.cloned.1.call-start = ((), (), s32[]{:S(2)}) async-start(), calls=%async_computation.15 | async-start | bytes 5308416 | tf_op jit(solution)/shard_map/reduce_scatter | solution.py:248
  468.4 10.1 copy-start.44
  468.4 10.1 copy-start.45
  478.5 9.6 copy-start.46
  497.8 101.1 %copy-start.7 = (bf16[128,2304]{1,0:T(8,128)(2,1)S(1)}, bf16[128,2304]{1,0:T(8,128)(2,1)}, u32[]{:S(2)}) copy-start(bf16[128,2304]{1,0:T(8,128)(2,1)} %param.16) | copy-start | bytes 1769476
  497.8 186.2 %all-gather.19.cloned.1.call-start = ((), (), s32[]{:S(2)}) async-start(), calls=%async_computation.16 | async-start | bytes 5308416 | tf_op jit(solution)/shard_map/all_gather | solution.py:262
  603.6 210.4 %reduce-scatter.11.cloned.1.call-start = ((), (), s32[]{:S(2)}) async-start(), calls=%async_computation.17 | async-start | bytes 5308416 | tf_op jit(solution)/shard_map/reduce_scatter | solution.py:271
  698.9 10.5 copy-start.49
  698.9 10.5 copy-start.47
  720.0 175.5 %reduce-scatter.13.cloned.1.call-start = ((), (), s32[]{:S(2)}) async-start(), calls=%async_computation.18 | async-start | bytes 2621440 | tf_op jit(solution)/shard_map/reduce_scatter | solution.py:346
  819.7 6.5 copy-start.34
  824.7 14.9 %collective-permute-start.2 = (bf16[128,2304]{1,0:T(8,128)(2,1)S(1)}, bf16[128,2304]{1,0:T(8,128)(2,1)S(1)}, u32[]{:S(2)}, u32[]{:S(2)}) collective-permute-start(bf16[128,2304]{1,0:T(8,128)(2,1)S(1)} %subtract_convert_fusion), channel_id=1, source_target_pairs={{0,1},{1,0},{2,3},{3,2},{4,5},{5,4},{6,7},{7,6},{8,9},{9,8},{10,11... | collective-permute-start | bytes 1769480 | tf_op jit(solution)/shard_map/ppermute | solution.py:60
  826.2 18.0 %copy-start.13 = (pred[256,1024]{0,1:T(8,128)(4,1)S(1)}, pred[256,1024]{0,1:T(8,128)(4,1)}, u32[]{:S(2)}) copy-start(pred[256,1024]{0,1:T(8,128)(4,1)} %copy-done.12) | copy-start | bytes 786436
  864.0 31.5 %copy-start.11 = (bf16[128,2304]{1,0:T(8,128)(2,1)S(1)}, bf16[128,2304]{1,0:T(8,128)(2,1)}, u32[]{:S(2)}) copy-start(bf16[128,2304]{1,0:T(8,128)(2,1)} %copy-done.10) | copy-start | bytes 1769476
  864.0 31.5 %copy-start.15 = (bf16[128,2304]{1,0:T(8,128)(2,1)S(1)}, bf16[128,2304]{1,0:T(8,128)(2,1)}, u32[]{:S(2)}) copy-start(bf16[128,2304]{1,0:T(8,128)(2,1)} %copy-done.14) | copy-start | bytes 1769476
  864.0 149.2 %reduce-scatter.15.cloned.1.call-start = ((), (), s32[]{:S(2)}) async-start(), calls=%async_computation.19 | async-start | bytes 10027008 | tf_op jit(solution)/shard_map/reduce_scatter | solution.py:354
  901.8 233.7 %reduce-scatter.19.cloned.1.call-start = ((), (), s32[]{:S(2)}) async-start(), calls=%async_computation.21 | async-start | bytes 19906560 | tf_op jit(solution)/shard_map/reduce_scatter | solution.py:286
  902.1 9.1 copy-start.48
  902.1 18.4 %slice-start = ((s8[4718592]{0:T(1024)(128)(4,1)}), s8[4194304]{0:T(1024)(128)(4,1)S(1)}, s32[]{:S(2)}) async-start(s8[4718592]{0:T(1024)(128)(4,1)} %bitcast.307), calls=%async_computation.22 | async-start | bytes 8388608
  911.2 9.3 slice-start.1
  911.2 9.3 copy-start.50
  971.2 310.3 %reduce-scatter.17.cloned.1.call-start = ((), (), s32[]{:S(2)}) async-start(), calls=%async_computation.20 | async-start | bytes 5013504 | tf_op jit(solution)/shard_map/reduce_scatter | solution.py:313
  1015.1 125.3 %copy-start.20 = (bf16[256,2,2,256]{0,3,2,1:T(8,128)(2,1)S(1)}, bf16[256,2,2,256]{0,3,2,1:T(8,128)(2,1)}, u32[]{:S(2)}) copy-start(bf16[256,2,2,256]{0,3,2,1:T(8,128)(2,1)} %reduce-scatter.13.cloned.1.call-done) | copy-start | bytes 1572868
  1015.1 125.3 %copy-start.21 = (bf16[2,256,2,256]{3,1,2,0:T(8,128)(2,1)S(1)}, bf16[2,256,2,256]{3,1,2,0:T(8,128)(2,1)}, u32[]{:S(2)}) copy-start(bf16[2,256,2,256]{3,1,2,0:T(8,128)(2,1)} %fusion.62) | copy-start | bytes 1572868
  1135.5 150.7 %all-to-all-start.3 = ((bf16[4,144,3456]{2,1,0:T(8,128)(2,1)}), bf16[4,144,3456]{2,1,0:T(8,128)(2,1)}, u32[]{:S(2)}, u32[]{:S(2)}) async-start(bf16[4,144,3456]{2,1,0:T(8,128)(2,1)} %bitcast.271), calls=%async_computation.8 | async-start | bytes 7962624 | tf_op jit(solution)/shard_map/all_to_all | solution.py:287
  1140.4 9.5 copy-start.29
  1140.4 9.5 copy-start.30
  1140.4 9.5 copy-start.31
  1140.4 22.9 %copy-start.1 = (bf16[128,2304]{1,0:T(8,128)(2,1)S(1)}, bf16[128,2304]{1,0:T(8,128)(2,1)}, u32[]{:S(2)}) copy-start(bf16[128,2304]{1,0:T(8,128)(2,1)} %param.15) | copy-start | bytes 1769476
  1140.4 22.9 %copy-start.27 = (f32[2304]{0:T(1024)S(1)}, f32[2304]{0:T(1024)}, u32[]{:S(2)}) copy-start(f32[2304]{0:T(1024)} %copy-done.26) | copy-start | bytes 27652
  1140.4 22.9 %copy-start.36 = (f32[128]{0:T(128)S(1)}, f32[128]{0:T(128)}, u32[]{:S(2)}) copy-start(f32[128]{0:T(128)} %copy-done.35) | copy-start | bytes 1540
  1140.5 138.3 %copy-start.42 = (f32[128]{0:T(128)S(1)}, f32[128]{0:T(128)}, u32[]{:S(2)}) copy-start(f32[128]{0:T(128)} %get-tuple-element.50) | copy-start | bytes 1540
  1148.3 15.0 %collective-permute-start.3 = (bf16[128,2304]{1,0:T(8,128)(2,1)S(1)}, bf16[128,2304]{1,0:T(8,128)(2,1)S(1)}, u32[]{:S(2)}, u32[]{:S(2)}) collective-permute-start(bf16[128,2304]{1,0:T(8,128)(2,1)S(1)} %slice.189), channel_id=1, source_target_pairs={{0,1},{1,0},{2,3},{3,2},{4,5},{5,4},{6,7},{7,6},{8,9},{9,8},{10,11... | collective-permute-start | bytes 1769480 | tf_op jit(solution)/shard_map/ppermute | solution.py:69
  (22 other events, 54.1 us)
Sparse Core Ops, SparseCore 0:
  21.2 81.3 all-gather.8
  113.1 18.5 all-gather.10
  134.1 53.1 all-gather.12
  214.0 140.5 all-gather.14
  369.5 98.8 all-gather.16
  497.9 95.6 reduce-scatter.8
  603.7 80.2 all-gather.18
  720.2 93.8 reduce-scatter.10
  864.1 31.3 reduce-scatter.12
  901.9 111.2 reduce-scatter.14
  1015.8 119.6 reduce-scatter.18
  1139.2 119.6 reduce-scatter.16
